TPU v7x, 32 devices: a whole 2x2x4 slice. The times are simulated.
32 devices in a mesh: tm: 4 (over y, core), dom: 8 (over z, x).
Axes of the slice: x: 2, y: 2, z: 4, core: 2. Of those that a mesh axis runs over, the one named last changes fastest.
Arguments:
- particles: float32 [4, 64, 4096], P('tm', None, 'dom'), may hold values from -12 to 12, as said below
- noise: float32 [4, 64, 4096], P('tm', None, 'dom'), may hold values from -6 to 6
Outputs:
- advanced: float32 [4, 64, 4096], P('tm', None, 'dom')
Inputs may be any that keep to these rules, and one draw needn't show every extreme that they name: `particles`: positions of cells in principal components, each time point about a shifted centre.
All inputs are finite; a program needn't handle non-finite values.
Results may differ from a plain program's by a relative error of at most 0.012.
The roundings to bfloat16 on the way count: a program that leaves them out, or rounds other values in their place, can miss the bound.
Values may be sent and summed in bfloat16 or wider, within the bound.
A program may use at most 64 MiB of HBM per device.

v0:
```python
import math
import jax
import jax.numpy as jnp
from jax import lax
from jax.sharding import PartitionSpec as P

SWEEPS = 2
EPS = 4.0
STEP = 0.5
TEMP = 0.05


def passed_along(value, axis, steps):
    count = lax.axis_size(axis)
    leading, last = (max(0, -steps), min(count, count - steps))
    return lax.ppermute(value, axis, [(source, source + steps) for source in range(leading, last)])


def col_tiles(targets, potential):
    features = targets.shape[0]
    col_count = targets.shape[1]
    tile_width = math.gcd(col_count, 1024)
    tile_count = col_count // tile_width
    tiles = targets.reshape(features, tile_count, tile_width).transpose(1, 0, 2)
    return (tiles, potential.reshape(tile_count, tile_width))


def tile_scores(sources, target_tile, pot_tile):
    products = lax.dot_general(
        sources, target_tile, (((0,), (0,)), ((), ())), preferred_element_type=jnp.float32
    )
    return (products + pot_tile[None, :]) / EPS


def log_totals(sources, tiles, pot_tiles):
    row_count = sources.shape[1]

    def log_advance(carry, pieces):
        highest, totals = carry
        scores = tile_scores(sources, pieces[0], pieces[1])
        merged = jnp.maximum(highest, jnp.max(scores, axis=1))
        totals = totals * jnp.exp(highest - merged) + jnp.sum(
            jnp.exp(scores - merged[:, None]), axis=1
        )
        return ((merged, totals), None)

    start = (jnp.full((row_count,), -jnp.inf, jnp.float32), jnp.zeros((row_count,), jnp.float32))
    (highest, totals), unused = lax.scan(log_advance, start, (tiles, pot_tiles))
    return (highest, totals)


def update(sources, targets, potential):
    tiles, pot_tiles = col_tiles(targets, potential)
    highest, totals = log_totals(sources, tiles, pot_tiles)
    result = -EPS * (highest + jnp.log(totals)) + EPS * math.log(targets.shape[1])
    return (result, highest, totals)


def barycentre(sources, targets, potential, highest, totals):
    tiles, pot_tiles = col_tiles(targets, potential)

    def barycentre_advance(summed, pieces):
        scores = tile_scores(sources, pieces[0], pieces[1])
        weights = (jnp.exp(scores - highest[:, None]) / totals[:, None]).astype(jnp.bfloat16)
        summed = summed + lax.dot_general(
            pieces[0], weights, (((1,), (1,)), ((), ())), preferred_element_type=jnp.float32
        )
        return (summed, None)

    start = jnp.zeros((targets.shape[0], sources.shape[1]), jnp.float32)
    summed, unused = lax.scan(barycentre_advance, start, (tiles, pot_tiles))
    return summed


def neighbours(own_block):
    gathered = lax.all_gather(own_block, "dom", axis=1, tiled=True)
    next_all = passed_along(gathered, "tm", -1)
    prev_all = passed_along(gathered, "tm", 1)
    return (next_all, prev_all)


def potentials_from(values, offset):
    gathered = lax.all_gather(values, "dom", axis=0, tiled=True)
    return passed_along(gathered, "tm", offset)


def per_device(particles, noise):
    points = particles[0]
    rounded = points.astype(jnp.bfloat16)
    next_all, prev_all = neighbours(rounded)
    time_index = lax.axis_index("tm")
    last_time = lax.axis_size("tm") - 1
    next_pot = -0.5 * jnp.sum(jnp.square(next_all.astype(jnp.float32)), axis=0)
    for sweep_index in range(SWEEPS):
        if sweep_index > 0:
            next_pot = potentials_from(target_pot, -1)
        source_pot, unused_high, unused_totals = update(rounded, next_all, next_pot)
        prev_pot = potentials_from(source_pot, 1)
        target_pot, prev_high, prev_totals = update(rounded, prev_all, prev_pot)
    next_pot = potentials_from(target_pot, -1)
    next_tiles, next_pot_tiles = col_tiles(next_all, next_pot)
    next_high, next_totals = log_totals(rounded, next_tiles, next_pot_tiles)
    bary_next = barycentre(rounded, next_all, next_pot, next_high, next_totals)
    bary_prev = barycentre(rounded, prev_all, prev_pot, prev_high, prev_totals)
    pull_next = jnp.where(time_index < last_time, points - bary_next, 0.0)
    pull_prev = jnp.where(time_index > 0, points - bary_prev, 0.0)
    advanced = points - STEP * (pull_next + pull_prev) + math.sqrt(2.0 * STEP * TEMP) * noise[0]
    return advanced[None]


def solution(mesh):
    in_specs = (P("tm", None, "dom"), P("tm", None, "dom"))
    out_specs = P("tm", None, "dom")
    return jax.shard_map(
        per_device, mesh=mesh, in_specs=in_specs, out_specs=out_specs, check_vma=False
    )
```

profile of v0, /device:TPU:5, one launch (start us, length us, event | category | flops | bytes accessed | tf_op | source)
XLA Modules:
  0.0 191.1 jit_solution(3282749936282625119)
XLA Ops:
  0.0 0.9 bitcast_convert_fusion
  0.9 26.1 %all_gather.15 = bf16[64,4096]{1,0:T(8,128)(2,1)S(1)} all-gather(bf16[64,512]{1,0:T(8,128)(2,1)S(1)} %bitcast_convert_fusion), channel_id=1, replica_groups=mesh['tm'=4,'dom'=8] {'dom'}, dimensions={1}, use_global_device_ids=true | all-gather | bytes 589824 | tf_op jit(solution)/shard_map/all_gather | solution.py:76
  27.0 8.0 %collective-permute-start = (bf16[64,4096]{1,0:T(8,128)(2,1)S(1)}, bf16[64,4096]{1,0:T(8,128)(2,1)S(1)}, u32[]{:S(2)}, u32[]{:S(2)}) collective-permute-start(bf16[64,4096]{1,0:T(8,128)(2,1)S(1)} %all_gather.15), channel_id=1, source_target_pairs={{8,0},{16,8},{24,16},{9,1},{17,9},{25,17},{10,2},{18,10},{26,18},{... | collective-permute-start | bytes 1572872 | tf_op jit(solution)/shard_map/ppermute | solution.py:16
  35.1 1.3 collective-permute-start.1
  36.8 4.3 %while.87 = (s32[]{:T(128)}, f32[512]{0:T(512)S(1)}, f32[512]{0:T(512)S(1)}, bf16[4,64,1024]{2,1,0:T(8,128)(2,1)S(1)}, bf16[64,512]{1,0:T(8,128)(2,1)S(1)}, /*index=5*/f32[4,1024]{1,0:T(4,128)S(1)}, s32[]{:T(128)}, s32[]{:T(128)}) while((s32[]{:T(128)}, f32[512]{0:T(512)S(1)}, f32[512]{0:T(512)S(1)}, ...), condition=%wide.region_4.5_spmd.clone, body=%wide.region_1.4_spmd.clone.sunk | while | flops 70781440 | bytes 4434024 | solution.py:48
  37.3 0.5 exponential_reduce_fusion.10
  38.4 0.5 exponential_reduce_fusion.10
  39.0 0.5 fusion.92
  39.5 0.5 exponential_reduce_fusion.10
  40.0 0.5 fusion.92
  40.6 0.5 exponential_reduce_fusion.10
  41.1 21.5 %all-gather = f32[8,1,512]{2,1,0:T(1,128)S(1)} all-gather(f32[1,1,512]{2,1,0:T(1,128)S(1)} %bitcast.159), channel_id=1, replica_groups=mesh['tm'=4,'dom'=8] {'dom'}, dimensions={0}, use_global_device_ids=true | all-gather | bytes 18432 | tf_op jit(solution)/shard_map/all_gather | solution.py:83
  62.6 1.3 collective-permute-start.2
  63.9 1.1 copy.11
  65.0 9.9 %collective-permute-done.2 = f32[4096]{0:T(1024)S(1)} collective-permute-done((f32[4096]{0:T(1024)S(1)}, f32[4096]{0:T(1024)S(1)}, u32[]{:S(2)}, u32[]{:S(2)}) %collective-permute-start.2) | collective-permute-done | bytes 16416 | tf_op jit(solution)/shard_map/ppermute | solution.py:16
  75.0 4.3 %while.88 = (s32[]{:T(128)}, f32[512]{0:T(512)S(1)}, f32[512]{0:T(512)S(1)}, bf16[4,64,1024]{2,1,0:T(8,128)(2,1)S(1)}, bf16[64,512]{1,0:T(8,128)(2,1)S(1)}, /*index=5*/f32[4,1024]{1,0:T(4,128)S(1)}, s32[]{:T(128)}, s32[]{:T(128)}) while((s32[]{:T(128)}, f32[512]{0:T(512)S(1)}, f32[512]{0:T(512)S(1)}, ...), condition=%wide.region_8.9_spmd.clone, body=%wide.region_5.8_spmd.clone.sunk | while | flops 70781440 | bytes 4434024 | solution.py:48
  75.5 0.5 exponential_reduce_fusion.11
  76.6 0.5 exponential_reduce_fusion.11
  78.7 0.5 exponential_reduce_fusion.11
  79.3 21.5 %all-gather.1 = f32[8,1,512]{2,1,0:T(1,128)S(1)} all-gather(f32[1,1,512]{2,1,0:T(1,128)S(1)} %bitcast.160), channel_id=1, replica_groups=mesh['tm'=4,'dom'=8] {'dom'}, dimensions={0}, use_global_device_ids=true | all-gather | bytes 18432 | tf_op jit(solution)/shard_map/all_gather | solution.py:83
  100.8 9.0 %collective-permute-start.3 = (f32[4096]{0:T(1024)S(1)}, f32[4096]{0:T(1024)S(1)}, u32[]{:S(2)}, u32[]{:S(2)}) collective-permute-start(f32[4096]{0:T(1024)S(1)} %bitcast.158), channel_id=1, source_target_pairs={{8,0},{16,8},{24,16},{9,1},{17,9},{25,17},{10,2},{18,10},{26,18},{... | collective-permute-start | bytes 49160 | tf_op jit(solution)/shard_map/ppermute | solution.py:16
  109.8 0.8 collective-permute-done.3
  110.6 4.3 %while.89 = (s32[]{:T(128)}, f32[512]{0:T(512)S(1)}, f32[512]{0:T(512)S(1)}, bf16[4,64,1024]{2,1,0:T(8,128)(2,1)S(1)}, bf16[64,512]{1,0:T(8,128)(2,1)S(1)}, /*index=5*/f32[4,1024]{1,0:T(4,128)S(1)}, s32[]{:T(128)}, s32[]{:T(128)}) while((s32[]{:T(128)}, f32[512]{0:T(512)S(1)}, f32[512]{0:T(512)S(1)}, ...), condition=%wide.region_12.13_spmd.clone, body=%wide.region_9.12_spmd.clone.sunk | while | flops 70781440 | bytes 4434024 | solution.py:48
  111.1 0.5 exponential_reduce_fusion.12
  112.2 0.5 exponential_reduce_fusion.12
  114.4 0.5 exponential_reduce_fusion.12
  114.9 21.5 %all-gather.2 = f32[8,1,512]{2,1,0:T(1,128)S(1)} all-gather(f32[1,1,512]{2,1,0:T(1,128)S(1)} %bitcast.161), channel_id=1, replica_groups=mesh['tm'=4,'dom'=8] {'dom'}, dimensions={0}, use_global_device_ids=true | all-gather | bytes 18432 | tf_op jit(solution)/shard_map/all_gather | solution.py:83
  136.4 1.3 collective-permute-start.4
  137.8 6.4 %collective-permute-done.4 = f32[4096]{0:T(1024)S(1)} collective-permute-done((f32[4096]{0:T(1024)S(1)}, f32[4096]{0:T(1024)S(1)}, u32[]{:S(2)}, u32[]{:S(2)}) %collective-permute-start.4) | collective-permute-done | bytes 16416 | tf_op jit(solution)/shard_map/ppermute | solution.py:16
  144.2 4.3 %while.90 = (s32[]{:T(128)}, f32[512]{0:T(512)S(1)}, f32[512]{0:T(512)S(1)}, bf16[4,64,1024]{2,1,0:T(8,128)(2,1)S(1)}, bf16[64,512]{1,0:T(8,128)(2,1)S(1)}, /*index=5*/f32[4,1024]{1,0:T(4,128)S(1)}, s32[]{:T(128)}, s32[]{:T(128)}) while((s32[]{:T(128)}, f32[512]{0:T(512)S(1)}, f32[512]{0:T(512)S(1)}, ...), condition=%wide.region_16.17_spmd.clone, body=%wide.region_13.16_spmd.clone.sunk | while | flops 70781440 | bytes 4434024 | solution.py:48
  144.8 0.5 exponential_reduce_fusion.13
  145.8 0.5 exponential_reduce_fusion.13
  146.9 0.5 exponential_reduce_fusion.13
  148.5 21.5 %all-gather.3 = f32[8,1,512]{2,1,0:T(1,128)S(1)} all-gather(f32[1,1,512]{2,1,0:T(1,128)S(1)} %bitcast.162), channel_id=1, replica_groups=mesh['tm'=4,'dom'=8] {'dom'}, dimensions={0}, use_global_device_ids=true | all-gather | bytes 18432 | tf_op jit(solution)/shard_map/all_gather | solution.py:83
  170.0 9.0 %collective-permute-start.5 = (f32[4096]{0:T(1024)S(1)}, f32[4096]{0:T(1024)S(1)}, u32[]{:S(2)}, u32[]{:S(2)}) collective-permute-start(f32[4096]{0:T(1024)S(1)} %bitcast.155), channel_id=1, source_target_pairs={{8,0},{16,8},{24,16},{9,1},{17,9},{25,17},{10,2},{18,10},{26,18},{... | collective-permute-start | bytes 49160 | tf_op jit(solution)/shard_map/ppermute | solution.py:16
  179.0 3.5 %while.93 = (s32[]{:T(128)}, f32[64,512]{1,0:T(8,128)S(1)}, bf16[4,64,1024]{2,1,0:T(8,128)(2,1)S(1)}, bf16[64,512]{1,0:T(8,128)(2,1)S(1)}, f32[4,1024]{1,0:T(4,1...) while((s32[]{:T(128)}, f32[64,512]{1,0:T(8,128)S(1)}, ...), condition=%wide.region_24.25_spmd.clone, body=%wide.region_23.24_spmd.clone.sunk | while | flops 136904704 | bytes 607339 | solution.py:71
  179.1 0.8 fusion.113
  179.9 0.8 fusion.113
  180.8 0.8 fusion.113
  181.7 0.8 fusion.113
  182.6 4.3 %while.91 = (s32[]{:T(128)}, f32[512]{0:T(512)S(1)}, f32[512]{0:T(512)S(1)}, bf16[4,64,1024]{2,1,0:T(8,128)(2,1)S(1)}, bf16[64,512]{1,0:T(8,128)(2,1)S(1)}, /*index=5*/f32[4,1024]{1,0:T(4,128)S(1)}, s32[]{:T(128)}, s32[]{:T(128)}) while((s32[]{:T(128)}, f32[512]{0:T(512)S(1)}, f32[512]{0:T(512)S(1)}, ...), condition=%wide.region_20.21_spmd.clone, body=%wide.region_17.20_spmd.clone.sunk | while | flops 70781440 | bytes 4434024 | solution.py:48
  182.6 0.5 fusion.104
  186.9 3.5 %while.92 = (s32[]{:T(128)}, f32[64,512]{1,0:T(8,128)S(1)}, bf16[4,64,1024]{2,1,0:T(8,128)(2,1)S(1)}, bf16[64,512]{1,0:T(8,128)(2,1)S(1)}, f32[4,1024]{1,0:T(4,1...) while((s32[]{:T(128)}, f32[64,512]{1,0:T(8,128)S(1)}, ...), condition=%wide.region_22.23_spmd.clone, body=%wide.region_21.22_spmd.clone.sunk | while | flops 136904704 | bytes 607339 | solution.py:71
  186.9 0.8 fusion.109
  187.8 0.8 fusion.109
  188.7 0.8 fusion.109
  189.5 0.8 fusion.109
  190.4 0.7 fusion.56
  (143 shorter events, 13.1 us)
Async XLA Ops:
  27.0 9.5 %collective-permute-start = (bf16[64,4096]{1,0:T(8,128)(2,1)S(1)}, bf16[64,4096]{1,0:T(8,128)(2,1)S(1)}, u32[]{:S(2)}, u32[]{:S(2)}) collective-permute-start(bf16[64,4096]{1,0:T(8,128)(2,1)S(1)} %all_gather.15), channel_id=1, source_target_pairs={{8,0},{16,8},{24,16},{9,1},{17,9},{25,17},{10,2},{18,10},{26,18},{... | collective-permute-start | bytes 1572872 | tf_op jit(solution)/shard_map/ppermute | solution.py:16
  35.1 28.8 %collective-permute-start.1 = (bf16[64,4096]{1,0:T(8,128)(2,1)S(1)}, bf16[64,4096]{1,0:T(8,128)(2,1)}, u32[]{:S(2)}, u32[]{:S(2)}) collective-permute-start(bf16[64,4096]{1,0:T(8,128)(2,1)S(1)} %all_gather.15), channel_id=1, source_target_pairs={{0,8},{8,16},{16,24},{1,9},{9,17},{17,25},{2,10},{10,18},{18,26},{... | collective-permute-start | bytes 1572872 | tf_op jit(solution)/shard_map/ppermute | solution.py:16
  62.6 12.3 %collective-permute-start.2 = (f32[4096]{0:T(1024)S(1)}, f32[4096]{0:T(1024)S(1)}, u32[]{:S(2)}, u32[]{:S(2)}) collective-permute-start(f32[4096]{0:T(1024)S(1)} %bitcast.157), channel_id=1, source_target_pairs={{0,8},{8,16},{16,24},{1,9},{9,17},{17,25},{2,10},{10,18},{18,26},{... | collective-permute-start | bytes 49160 | tf_op jit(solution)/shard_map/ppermute | solution.py:16
  100.8 9.8 %collective-permute-start.3 = (f32[4096]{0:T(1024)S(1)}, f32[4096]{0:T(1024)S(1)}, u32[]{:S(2)}, u32[]{:S(2)}) collective-permute-start(f32[4096]{0:T(1024)S(1)} %bitcast.158), channel_id=1, source_target_pairs={{8,0},{16,8},{24,16},{9,1},{17,9},{25,17},{10,2},{18,10},{26,18},{... | collective-permute-start | bytes 49160 | tf_op jit(solution)/shard_map/ppermute | solution.py:16
  136.4 7.8 %collective-permute-start.4 = (f32[4096]{0:T(1024)S(1)}, f32[4096]{0:T(1024)S(1)}, u32[]{:S(2)}, u32[]{:S(2)}) collective-permute-start(f32[4096]{0:T(1024)S(1)} %bitcast.156), channel_id=1, source_target_pairs={{0,8},{8,16},{16,24},{1,9},{9,17},{17,25},{2,10},{10,18},{18,26},{... | collective-permute-start | bytes 49160 | tf_op jit(solution)/shard_map/ppermute | solution.py:16
  170.0 12.5 %collective-permute-start.5 = (f32[4096]{0:T(1024)S(1)}, f32[4096]{0:T(1024)S(1)}, u32[]{:S(2)}, u32[]{:S(2)}) collective-permute-start(f32[4096]{0:T(1024)S(1)} %bitcast.155), channel_id=1, source_target_pairs={{8,0},{16,8},{24,16},{9,1},{17,9},{25,17},{10,2},{18,10},{26,18},{... | collective-permute-start | bytes 49160 | tf_op jit(solution)/shard_map/ppermute | solution.py:16
  186.9 3.5 %copy-start = (f32[1,64,512]{2,1,0:T(8,128)S(1)}, f32[1,64,512]{2,1,0:T(8,128)}, u32[]{:S(2)}) copy-start(f32[1,64,512]{2,1,0:T(8,128)} %param.16) | copy-start | bytes 393220
  186.9 3.5 %copy-start.1 = (f32[1,64,512]{2,1,0:T(8,128)S(1)}, f32[1,64,512]{2,1,0:T(8,128)}, u32[]{:S(2)}) copy-start(f32[1,64,512]{2,1,0:T(8,128)} %param.17) | copy-start | bytes 393220
where the time goes:
time: 191 us
  blocking collectives  112 us (59%)
  starting transfers between devices  29.8 us (16%)
  waiting for transfers between devices  17.3 us (9%)
  matrix products  16.5 us (9%)
  other arithmetic  12.2 us (6%)
    all_gather x4, blocking collectives, potentials_from(): gathered = lax.all_gather(values, 'dom', axis=0, tiled=True)  86.1 us
    ppermute x6, starting transfers between devices, passed_along(): lax.ppermute(value, axis, [(source, source + steps) for source in range(l...  29.8 us
    all_gather x1, blocking collectives, neighbours(): gathered = lax.all_gather(own_block, 'dom', axis=1, tiled=True)  26.1 us
    ppermute x6, waiting for transfers between devices, passed_along(): lax.ppermute(value, axis, [(source, source + steps) for source in range(l...  17.3 us
    reduce_sum x20, other arithmetic, log_advance(): jnp.sum(jnp.exp(scores - merged[:, None]), axis=1)  9.89 us
    dot_general x20, matrix products, tile_scores(): lax.dot_general(sources, target_tile, (((0,), (0,)), ((), ())), preferred...  9.87 us
    dot_general x8, matrix products, barycentre_advance(): lax.dot_general(pieces[0], weights, (((1,), (1,)), ((), ())), preferred_e...  6.65 us
  transfers between devices with their start and end apart: 6, of which 4 were waited for; matrix products, arithmetic and copies ran while one was open for 5% of the time, Pallas kernels for 0%

commit v1 on v0

--- a/solution.py
+++ b/solution.py
@@ -73,7 +73,13 @@
 
 
 def neighbours(own_block):
-    gathered = lax.all_gather(own_block, "dom", axis=1, tiled=True)
+    devices = lax.axis_size("dom")
+    held, tiles_2 = (own_block, [own_block])
+    for _ in range(devices - 1):
+        held = lax.ppermute(held, "dom", [(i, (i + 1) % devices) for i in range(devices)])
+        tiles_2.insert(0, held)
+    line = jnp.concatenate(tiles_2, axis=1)
+    gathered = jnp.roll(line, (lax.axis_index("dom") + 1) * own_block.shape[1], axis=1)
     next_all = passed_along(gathered, "tm", -1)
     prev_all = passed_along(gathered, "tm", 1)
     return (next_all, prev_all)

time: 191 us -> 217 us (1.14)
  waiting for transfers between devices: 17.3 us -> 57.9 us
  blocking collectives: 112 us -> 86.1 us
  matrix products: 16.5 us -> 21.8 us
  starting transfers between devices: 29.8 us -> 33.5 us
    ppermute x0 -> x7, waiting for transfers between devices: none -> 40.2 us  [neighbours(): lax.ppermute(held, 'dom', [(i, (i + 1) % devices) for i in range(devices)])]
    all_gather x1 -> x0, blocking collectives: 26.1 us -> none  [neighbours(): gathered = lax.all_gather(own_block, 'dom', axis=1, tiled=True)]
    dot_general x8, matrix products: 6.65 us -> 12 us  [barycentre_advance(): lax.dot_general(pieces[0], weights, (((1,), (1,)), ((), ())), preferred_e...]
    ppermute x6, starting transfers between devices: 29.8 us -> 32.2 us  [passed_along(): lax.ppermute(value, axis, [(source, source + steps) for source in range(l...]
  transfers between devices with their start and end apart: 6 -> 13, of which waited for: 4 -> 11; matrix products, arithmetic and copies ran while one was open for 5% -> 6% of each run, Pallas kernels for 0% -> 0%
where the time goes in v1:
time: 217 us; the launch traced here: 216 us
  blocking collectives  86.1 us (40%)
  waiting for transfers between devices  57.9 us (27%)
  starting transfers between devices  33.5 us (15%)
  matrix products  21.8 us (10%)
  other arithmetic  13.2 us (6%)
  local copies, waits for them, and re-layouts  2.41 us (1%)
    all_gather x4, blocking collectives, potentials_from(): gathered = lax.all_gather(values, 'dom', axis=0, tiled=True)  86.1 us
    ppermute x7, waiting for transfers between devices, neighbours(): lax.ppermute(held, 'dom', [(i, (i + 1) % devices) for i in range(devices)])  40.2 us
    ppermute x6, starting transfers between devices, passed_along(): lax.ppermute(value, axis, [(source, source + steps) for source in range(l...  32.2 us
    ppermute x6, waiting for transfers between devices, passed_along(): lax.ppermute(value, axis, [(source, source + steps) for source in range(l...  17.7 us
    dot_general x8, matrix products, barycentre_advance(): lax.dot_general(pieces[0], weights, (((1,), (1,)), ((), ())), preferred_e...  12 us
    reduce_sum x20, other arithmetic, log_advance(): jnp.sum(jnp.exp(scores - merged[:, None]), axis=1)  9.88 us
    dot_general x20, matrix products, tile_scores(): lax.dot_general(sources, target_tile, (((0,), (0,)), ((), ())), preferred...  9.87 us
  transfers between devices with their start and end apart: 13, of which 11 were waited for; matrix products, arithmetic and copies ran while one was open for 6% of the time, Pallas kernels for 0%

profile of v1, /device:TPU:5, one launch (start us, length us, event | category | flops | bytes accessed | tf_op | source)
XLA Modules:
  0.0 216.4 jit_solution(6444887649361624487)
XLA Ops:
  0.0 1.0 bitcast_convert_fusion
  1.0 1.3 collective-permute-start
  2.3 4.7 %collective-permute-done = bf16[64,512]{1,0:T(8,128)(2,1)S(1)} collective-permute-done((bf16[64,512]{1,0:T(8,128)(2,1)S(1)}, bf16[64,512]{1,0:T(8,128)(2,1)S(1)}, u32[]{:S(2)}, u32[]{:S(2)}) %collective-permute-start) | collective-permute-done | bytes 65568 | tf_op jit(solution)/shard_map/ppermute | solution.py:79
  7.0 5.8 %collective-permute-done.1 = bf16[64,512]{1,0:T(8,128)(2,1)S(1)} collective-permute-done((bf16[64,512]{1,0:T(8,128)(2,1)S(1)}, bf16[64,512]{1,0:T(8,128)(2,1)S(1)}, u32[]{:S(2)}, u32[]{:S(2)}) %collective-permute-start.1) | collective-permute-done | bytes 65568 | tf_op jit(solution)/shard_map/ppermute | solution.py:79
  12.8 5.8 %collective-permute-done.2 = bf16[64,512]{1,0:T(8,128)(2,1)S(1)} collective-permute-done((bf16[64,512]{1,0:T(8,128)(2,1)S(1)}, bf16[64,512]{1,0:T(8,128)(2,1)S(1)}, u32[]{:S(2)}, u32[]{:S(2)}) %collective-permute-start.2) | collective-permute-done | bytes 65568 | tf_op jit(solution)/shard_map/ppermute | solution.py:79
  18.6 5.8 %collective-permute-done.3 = bf16[64,512]{1,0:T(8,128)(2,1)S(1)} collective-permute-done((bf16[64,512]{1,0:T(8,128)(2,1)S(1)}, bf16[64,512]{1,0:T(8,128)(2,1)S(1)}, u32[]{:S(2)}, u32[]{:S(2)}) %collective-permute-start.3) | collective-permute-done | bytes 65568 | tf_op jit(solution)/shard_map/ppermute | solution.py:79
  24.4 5.8 %collective-permute-done.4 = bf16[64,512]{1,0:T(8,128)(2,1)S(1)} collective-permute-done((bf16[64,512]{1,0:T(8,128)(2,1)S(1)}, bf16[64,512]{1,0:T(8,128)(2,1)S(1)}, u32[]{:S(2)}, u32[]{:S(2)}) %collective-permute-start.4) | collective-permute-done | bytes 65568 | tf_op jit(solution)/shard_map/ppermute | solution.py:79
  30.2 6.5 %collective-permute-done.5 = bf16[64,512]{1,0:T(8,128)(2,1)S(1)} collective-permute-done((bf16[64,512]{1,0:T(8,128)(2,1)S(1)}, bf16[64,512]{1,0:T(8,128)(2,1)S(1)}, u32[]{:S(2)}, u32[]{:S(2)}) %collective-permute-start.5) | collective-permute-done | bytes 65568 | tf_op jit(solution)/shard_map/ppermute | solution.py:79
  36.7 5.8 %collective-permute-done.6 = bf16[64,512]{1,0:T(8,128)(2,1)S(1)} collective-permute-done((bf16[64,512]{1,0:T(8,128)(2,1)S(1)}, bf16[64,512]{1,0:T(8,128)(2,1)S(1)}, u32[]{:S(2)}, u32[]{:S(2)}) %collective-permute-start.6) | collective-permute-done | bytes 65568 | tf_op jit(solution)/shard_map/ppermute | solution.py:79
  42.6 0.9 constant_dynamic-update-slice_fusion.8
  43.6 0.8 constant_dynamic-slice_fusion.7
  44.5 10.4 %collective-permute-start.7 = (bf16[64,4096]{1,0:T(8,128)(2,1)}, bf16[64,4096]{1,0:T(8,128)(2,1)S(1)}, u32[]{:S(2)}, u32[]{:S(2)}) collective-permute-start(bf16[64,4096]{1,0:T(8,128)(2,1)} %constant_dynamic-slice_fusion.7), channel_id=1, source_target_pairs={{8,0},{16,8},{24,16},{9,1},{17,9},{25,17},{10,2},{18,10},{26,18},{... | collective-permute-start | bytes 1572872 | tf_op jit(solution)/shard_map/ppermute | solution.py:16
  54.9 1.3 collective-permute-start.8
  56.8 4.3 %while.87 = (s32[]{:T(128)}, f32[512]{0:T(512)S(1)}, f32[512]{0:T(512)S(1)}, bf16[4,64,1024]{2,1,0:T(8,128)(2,1)S(1)}, bf16[64,512]{1,0:T(8,128)(2,1)S(1)}, /*index=5*/f32[4,1024]{1,0:T(4,128)S(1)}, s32[]{:T(128)}, s32[]{:T(128)}) while((s32[]{:T(128)}, f32[512]{0:T(512)S(1)}, f32[512]{0:T(512)S(1)}, ...), condition=%wide.region_4.5_spmd.clone, body=%wide.region_1.4_spmd.clone.sunk | while | flops 70781440 | bytes 4434024 | solution.py:48
  57.3 0.5 exponential_reduce_fusion.10
  60.6 0.5 exponential_reduce_fusion.10
  61.1 21.5 %all-gather = f32[8,1,512]{2,1,0:T(1,128)S(1)} all-gather(f32[1,1,512]{2,1,0:T(1,128)S(1)} %bitcast.163), channel_id=1, replica_groups=mesh['tm'=4,'dom'=8] {'dom'}, dimensions={0}, use_global_device_ids=true | all-gather | bytes 18432 | tf_op jit(solution)/shard_map/all_gather | solution.py:89
  82.6 1.3 collective-permute-start.9
  83.9 1.1 copy.11
  85.0 10.0 %collective-permute-done.9 = f32[4096]{0:T(1024)S(1)} collective-permute-done((f32[4096]{0:T(1024)S(1)}, f32[4096]{0:T(1024)S(1)}, u32[]{:S(2)}, u32[]{:S(2)}) %collective-permute-start.9) | collective-permute-done | bytes 16416 | tf_op jit(solution)/shard_map/ppermute | solution.py:16
  95.1 4.3 %while.88 = (s32[]{:T(128)}, f32[512]{0:T(512)S(1)}, f32[512]{0:T(512)S(1)}, bf16[4,64,1024]{2,1,0:T(8,128)(2,1)S(1)}, bf16[64,512]{1,0:T(8,128)(2,1)S(1)}, /*index=5*/f32[4,1024]{1,0:T(4,128)S(1)}, s32[]{:T(128)}, s32[]{:T(128)}) while((s32[]{:T(128)}, f32[512]{0:T(512)S(1)}, f32[512]{0:T(512)S(1)}, ...), condition=%wide.region_8.9_spmd.clone, body=%wide.region_5.8_spmd.clone.sunk | while | flops 70781440 | bytes 4434024 | solution.py:48
  97.8 0.5 exponential_reduce_fusion.11
  98.8 0.5 exponential_reduce_fusion.11
  99.4 21.5 %all-gather.1 = f32[8,1,512]{2,1,0:T(1,128)S(1)} all-gather(f32[1,1,512]{2,1,0:T(1,128)S(1)} %bitcast.164), channel_id=1, replica_groups=mesh['tm'=4,'dom'=8] {'dom'}, dimensions={0}, use_global_device_ids=true | all-gather | bytes 18432 | tf_op jit(solution)/shard_map/all_gather | solution.py:89
  120.9 9.0 %collective-permute-start.10 = (f32[4096]{0:T(1024)S(1)}, f32[4096]{0:T(1024)S(1)}, u32[]{:S(2)}, u32[]{:S(2)}) collective-permute-start(f32[4096]{0:T(1024)S(1)} %bitcast.162), channel_id=1, source_target_pairs={{8,0},{16,8},{24,16},{9,1},{17,9},{25,17},{10,2},{18,10},{26,18},{... | collective-permute-start | bytes 49160 | tf_op jit(solution)/shard_map/ppermute | solution.py:16
  129.9 0.8 collective-permute-done.10
  130.7 4.3 %while.89 = (s32[]{:T(128)}, f32[512]{0:T(512)S(1)}, f32[512]{0:T(512)S(1)}, bf16[4,64,1024]{2,1,0:T(8,128)(2,1)S(1)}, bf16[64,512]{1,0:T(8,128)(2,1)S(1)}, /*index=5*/f32[4,1024]{1,0:T(4,128)S(1)}, s32[]{:T(128)}, s32[]{:T(128)}) while((s32[]{:T(128)}, f32[512]{0:T(512)S(1)}, f32[512]{0:T(512)S(1)}, ...), condition=%wide.region_12.13_spmd.clone, body=%wide.region_9.12_spmd.clone.sunk | while | flops 70781440 | bytes 4434024 | solution.py:48
  132.3 0.5 exponential_reduce_fusion.12
  133.4 0.5 exponential_reduce_fusion.12
  135.0 21.5 %all-gather.2 = f32[8,1,512]{2,1,0:T(1,128)S(1)} all-gather(f32[1,1,512]{2,1,0:T(1,128)S(1)} %bitcast.165), channel_id=1, replica_groups=mesh['tm'=4,'dom'=8] {'dom'}, dimensions={0}, use_global_device_ids=true | all-gather | bytes 18432 | tf_op jit(solution)/shard_map/all_gather | solution.py:89
  156.5 1.3 collective-permute-start.11
  157.9 6.4 %collective-permute-done.11 = f32[4096]{0:T(1024)S(1)} collective-permute-done((f32[4096]{0:T(1024)S(1)}, f32[4096]{0:T(1024)S(1)}, u32[]{:S(2)}, u32[]{:S(2)}) %collective-permute-start.11) | collective-permute-done | bytes 16416 | tf_op jit(solution)/shard_map/ppermute | solution.py:16
  164.3 4.3 %while.90 = (s32[]{:T(128)}, f32[512]{0:T(512)S(1)}, f32[512]{0:T(512)S(1)}, bf16[4,64,1024]{2,1,0:T(8,128)(2,1)S(1)}, bf16[64,512]{1,0:T(8,128)(2,1)S(1)}, /*index=5*/f32[4,1024]{1,0:T(4,128)S(1)}, s32[]{:T(128)}, s32[]{:T(128)}) while((s32[]{:T(128)}, f32[512]{0:T(512)S(1)}, f32[512]{0:T(512)S(1)}, ...), condition=%wide.region_16.17_spmd.clone, body=%wide.region_13.16_spmd.clone.sunk | while | flops 70781440 | bytes 4434024 | solution.py:48
  168.6 21.5 %all-gather.3 = f32[8,1,512]{2,1,0:T(1,128)S(1)} all-gather(f32[1,1,512]{2,1,0:T(1,128)S(1)} %bitcast.166), channel_id=1, replica_groups=mesh['tm'=4,'dom'=8] {'dom'}, dimensions={0}, use_global_device_ids=true | all-gather | bytes 18432 | tf_op jit(solution)/shard_map/all_gather | solution.py:89
  190.1 9.0 %collective-permute-start.12 = (f32[4096]{0:T(1024)S(1)}, f32[4096]{0:T(1024)S(1)}, u32[]{:S(2)}, u32[]{:S(2)}) collective-permute-start(f32[4096]{0:T(1024)S(1)} %bitcast.159), channel_id=1, source_target_pairs={{8,0},{16,8},{24,16},{9,1},{17,9},{25,17},{10,2},{18,10},{26,18},{... | collective-permute-start | bytes 49160 | tf_op jit(solution)/shard_map/ppermute | solution.py:16
  199.1 8.7 %while.93 = (s32[]{:T(128)}, f32[64,512]{1,0:T(8,128)}, bf16[4,64,1024]{2,1,0:T(8,128)(2,1)S(1)}, bf16[64,512]{1,0:T(8,128)(2,1)S(1)}, f32[4,1024]{1,0:T(4,128)S...) while((s32[]{:T(128)}, f32[64,512]{1,0:T(8,128)}, ...), condition=%wide.region_24.25_spmd.clone, body=%wide.region_23.24_spmd.clone.sunk | while | flops 136904704 | bytes 607339 | solution.py:71
  199.2 1.5 fusion.113
  200.7 2.4 %fusion.113 = f32[64,512]{1,0:T(8,128)} fusion(bf16[64,512]{1,0:T(8,128)(2,1)S(1)} %get-tuple-element.915, f32[512]{0:T(512)S(1)} %get-tuple-element.918, f32[512]{0:T(512)S(1)} %get-tuple-element.917, f32[1024]{0:T(1024)S(1)} %bitcast.157, f32[64,512]{1,0:T(8,128)} %get-tuple-element.904, bf16[4,64,1024]{2,1,0:T(8,128)(2,1)S(1)} %get-tuple-element.914, ...), kind=kOutput, calls=%fused_computation.69.clone.1 | convolution fusion | flops 136904704 | bytes 599041 | tf_op jit(solution)/shard_map/while/body/eval_jaxpr/dot_general | solution.py:65
  203.1 2.4 %fusion.113 = f32[64,512]{1,0:T(8,128)} fusion(bf16[64,512]{1,0:T(8,128)(2,1)S(1)} %get-tuple-element.915, f32[512]{0:T(512)S(1)} %get-tuple-element.918, f32[512]{0:T(512)S(1)} %get-tuple-element.917, f32[1024]{0:T(1024)S(1)} %bitcast.157, f32[64,512]{1,0:T(8,128)} %get-tuple-element.904, bf16[4,64,1024]{2,1,0:T(8,128)(2,1)S(1)} %get-tuple-element.914, ...), kind=kOutput, calls=%fused_computation.69.clone.1 | convolution fusion | flops 136904704 | bytes 599041 | tf_op jit(solution)/shard_map/while/body/eval_jaxpr/dot_general | solution.py:65
  205.5 2.4 %fusion.113 = f32[64,512]{1,0:T(8,128)} fusion(bf16[64,512]{1,0:T(8,128)(2,1)S(1)} %get-tuple-element.915, f32[512]{0:T(512)S(1)} %get-tuple-element.918, f32[512]{0:T(512)S(1)} %get-tuple-element.917, f32[1024]{0:T(1024)S(1)} %bitcast.157, f32[64,512]{1,0:T(8,128)} %get-tuple-element.904, bf16[4,64,1024]{2,1,0:T(8,128)(2,1)S(1)} %get-tuple-element.914, ...), kind=kOutput, calls=%fused_computation.69.clone.1 | convolution fusion | flops 136904704 | bytes 599041 | tf_op jit(solution)/shard_map/while/body/eval_jaxpr/dot_general | solution.py:65
  207.9 4.3 %while.91 = (s32[]{:T(128)}, f32[512]{0:T(512)S(1)}, f32[512]{0:T(512)S(1)}, bf16[4,64,1024]{2,1,0:T(8,128)(2,1)S(1)}, bf16[64,512]{1,0:T(8,128)(2,1)S(1)}, /*index=5*/f32[4,1024]{1,0:T(4,128)S(1)}, s32[]{:T(128)}, s32[]{:T(128)}) while((s32[]{:T(128)}, f32[512]{0:T(512)S(1)}, f32[512]{0:T(512)S(1)}, ...), condition=%wide.region_20.21_spmd.clone, body=%wide.region_17.20_spmd.clone.sunk | while | flops 70781440 | bytes 4434024 | solution.py:48
  211.1 0.5 fusion.104
  212.2 3.5 %while.92 = (s32[]{:T(128)}, f32[64,512]{1,0:T(8,128)S(1)}, bf16[4,64,1024]{2,1,0:T(8,128)(2,1)S(1)}, bf16[64,512]{1,0:T(8,128)(2,1)S(1)}, f32[4,1024]{1,0:T(4,1...) while((s32[]{:T(128)}, f32[64,512]{1,0:T(8,128)S(1)}, ...), condition=%wide.region_22.23_spmd.clone, body=%wide.region_21.22_spmd.clone.sunk | while | flops 136904704 | bytes 607339 | solution.py:71
  212.2 0.8 fusion.109
  213.1 0.8 fusion.109
  214.0 0.8 fusion.109
  214.8 0.8 fusion.109
  215.7 0.7 fusion.56
  (175 shorter events, 17.8 us)
Async XLA Ops:
  0.0 43.6 %copy-start = (f32[1,64,512]{2,1,0:T(8,128)S(1)}, f32[1,64,512]{2,1,0:T(8,128)}, u32[]{:S(2)}) copy-start(f32[1,64,512]{2,1,0:T(8,128)} %param.16) | copy-start | bytes 393220
  1.0 6.0 %collective-permute-start = (bf16[64,512]{1,0:T(8,128)(2,1)S(1)}, bf16[64,512]{1,0:T(8,128)(2,1)S(1)}, u32[]{:S(2)}, u32[]{:S(2)}) collective-permute-start(bf16[64,512]{1,0:T(8,128)(2,1)S(1)} %bitcast_convert_fusion), channel_id=1, source_target_pairs={{0,1},{1,2},{2,3},{3,4},{4,5},{5,6},{6,7},{7,0},{8,9},{9,10},{10,1... | collective-permute-start | bytes 196616 | tf_op jit(solution)/shard_map/ppermute | solution.py:79
  7.0 5.8 %collective-permute-start.1 = (bf16[64,512]{1,0:T(8,128)(2,1)S(1)}, bf16[64,512]{1,0:T(8,128)(2,1)S(1)}, u32[]{:S(2)}, u32[]{:S(2)}) collective-permute-start(bf16[64,512]{1,0:T(8,128)(2,1)S(1)} %collective-permute-done), channel_id=1, source_target_pairs={{0,1},{1,2},{2,3},{3,4},{4,5},{5,6},{6,7},{7,0},{8,9},{9,10},{10,1... | collective-permute-start | bytes 196616 | tf_op jit(solution)/shard_map/ppermute | solution.py:79
  12.8 5.8 %collective-permute-start.2 = (bf16[64,512]{1,0:T(8,128)(2,1)S(1)}, bf16[64,512]{1,0:T(8,128)(2,1)S(1)}, u32[]{:S(2)}, u32[]{:S(2)}) collective-permute-start(bf16[64,512]{1,0:T(8,128)(2,1)S(1)} %collective-permute-done.1), channel_id=1, source_target_pairs={{0,1},{1,2},{2,3},{3,4},{4,5},{5,6},{6,7},{7,0},{8,9},{9,10},{10,1... | collective-permute-start | bytes 196616 | tf_op jit(solution)/shard_map/ppermute | solution.py:79
  18.6 5.8 %collective-permute-start.3 = (bf16[64,512]{1,0:T(8,128)(2,1)S(1)}, bf16[64,512]{1,0:T(8,128)(2,1)S(1)}, u32[]{:S(2)}, u32[]{:S(2)}) collective-permute-start(bf16[64,512]{1,0:T(8,128)(2,1)S(1)} %collective-permute-done.2), channel_id=1, source_target_pairs={{0,1},{1,2},{2,3},{3,4},{4,5},{5,6},{6,7},{7,0},{8,9},{9,10},{10,1... | collective-permute-start | bytes 196616 | tf_op jit(solution)/shard_map/ppermute | solution.py:79
  24.4 5.8 %collective-permute-start.4 = (bf16[64,512]{1,0:T(8,128)(2,1)S(1)}, bf16[64,512]{1,0:T(8,128)(2,1)S(1)}, u32[]{:S(2)}, u32[]{:S(2)}) collective-permute-start(bf16[64,512]{1,0:T(8,128)(2,1)S(1)} %collective-permute-done.3), channel_id=1, source_target_pairs={{0,1},{1,2},{2,3},{3,4},{4,5},{5,6},{6,7},{7,0},{8,9},{9,10},{10,1... | collective-permute-start | bytes 196616 | tf_op jit(solution)/shard_map/ppermute | solution.py:79
  30.2 6.5 %collective-permute-start.5 = (bf16[64,512]{1,0:T(8,128)(2,1)S(1)}, bf16[64,512]{1,0:T(8,128)(2,1)S(1)}, u32[]{:S(2)}, u32[]{:S(2)}) collective-permute-start(bf16[64,512]{1,0:T(8,128)(2,1)S(1)} %collective-permute-done.4), channel_id=1, source_target_pairs={{0,1},{1,2},{2,3},{3,4},{4,5},{5,6},{6,7},{7,0},{8,9},{9,10},{10,1... | collective-permute-start | bytes 196616 | tf_op jit(solution)/shard_map/ppermute | solution.py:79
  36.7 5.8 %collective-permute-start.6 = (bf16[64,512]{1,0:T(8,128)(2,1)S(1)}, bf16[64,512]{1,0:T(8,128)(2,1)S(1)}, u32[]{:S(2)}, u32[]{:S(2)}) collective-permute-start(bf16[64,512]{1,0:T(8,128)(2,1)S(1)} %collective-permute-done.5), channel_id=1, source_target_pairs={{0,1},{1,2},{2,3},{3,4},{4,5},{5,6},{6,7},{7,0},{8,9},{9,10},{10,1... | collective-permute-start | bytes 196616 | tf_op jit(solution)/shard_map/ppermute | solution.py:79
  44.5 12.1 %collective-permute-start.7 = (bf16[64,4096]{1,0:T(8,128)(2,1)}, bf16[64,4096]{1,0:T(8,128)(2,1)S(1)}, u32[]{:S(2)}, u32[]{:S(2)}) collective-permute-start(bf16[64,4096]{1,0:T(8,128)(2,1)} %constant_dynamic-slice_fusion.7), channel_id=1, source_target_pairs={{8,0},{16,8},{24,16},{9,1},{17,9},{25,17},{10,2},{18,10},{26,18},{... | collective-permute-start | bytes 1572872 | tf_op jit(solution)/shard_map/ppermute | solution.py:16
  54.9 29.0 %collective-permute-start.8 = (bf16[64,4096]{1,0:T(8,128)(2,1)}, bf16[64,4096]{1,0:T(8,128)(2,1)}, u32[]{:S(2)}, u32[]{:S(2)}) collective-permute-start(bf16[64,4096]{1,0:T(8,128)(2,1)} %constant_dynamic-slice_fusion.7), channel_id=1, source_target_pairs={{0,8},{8,16},{16,24},{1,9},{9,17},{17,25},{2,10},{10,18},{18,26},{... | collective-permute-start | bytes 1572872 | tf_op jit(solution)/shard_map/ppermute | solution.py:16
  82.6 12.4 %collective-permute-start.9 = (f32[4096]{0:T(1024)S(1)}, f32[4096]{0:T(1024)S(1)}, u32[]{:S(2)}, u32[]{:S(2)}) collective-permute-start(f32[4096]{0:T(1024)S(1)} %bitcast.161), channel_id=1, source_target_pairs={{0,8},{8,16},{16,24},{1,9},{9,17},{17,25},{2,10},{10,18},{18,26},{... | collective-permute-start | bytes 49160 | tf_op jit(solution)/shard_map/ppermute | solution.py:16
  120.9 9.8 %collective-permute-start.10 = (f32[4096]{0:T(1024)S(1)}, f32[4096]{0:T(1024)S(1)}, u32[]{:S(2)}, u32[]{:S(2)}) collective-permute-start(f32[4096]{0:T(1024)S(1)} %bitcast.162), channel_id=1, source_target_pairs={{8,0},{16,8},{24,16},{9,1},{17,9},{25,17},{10,2},{18,10},{26,18},{... | collective-permute-start | bytes 49160 | tf_op jit(solution)/shard_map/ppermute | solution.py:16
  156.5 7.8 %collective-permute-start.11 = (f32[4096]{0:T(1024)S(1)}, f32[4096]{0:T(1024)S(1)}, u32[]{:S(2)}, u32[]{:S(2)}) collective-permute-start(f32[4096]{0:T(1024)S(1)} %bitcast.160), channel_id=1, source_target_pairs={{0,8},{8,16},{16,24},{1,9},{9,17},{17,25},{2,10},{10,18},{18,26},{... | collective-permute-start | bytes 49160 | tf_op jit(solution)/shard_map/ppermute | solution.py:16
  190.1 17.7 %collective-permute-start.12 = (f32[4096]{0:T(1024)S(1)}, f32[4096]{0:T(1024)S(1)}, u32[]{:S(2)}, u32[]{:S(2)}) collective-permute-start(f32[4096]{0:T(1024)S(1)} %bitcast.159), channel_id=1, source_target_pairs={{8,0},{16,8},{24,16},{9,1},{17,9},{25,17},{10,2},{18,10},{26,18},{... | collective-permute-start | bytes 49160 | tf_op jit(solution)/shard_map/ppermute | solution.py:16
  212.2 3.5 %copy-start.1 = (f32[1,64,512]{2,1,0:T(8,128)S(1)}, f32[1,64,512]{2,1,0:T(8,128)}, u32[]{:S(2)}) copy-start(f32[1,64,512]{2,1,0:T(8,128)} %param.17) | copy-start | bytes 393220
  212.2 3.5 %copy-start.2 = (f32[64,512]{1,0:T(8,128)S(1)}, f32[64,512]{1,0:T(8,128)}, u32[]{:S(2)}) copy-start(f32[64,512]{1,0:T(8,128)} %get-tuple-element.255) | copy-start | bytes 393220
